TPU v7x, 32 devices: a whole 2x2x4 slice. The times are simulated.
32 devices in a mesh: dom: 16 (over z, y, x), spin: 2 (over core).
Axes of the slice: x: 2, y: 2, z: 4, core: 2. Of those that a mesh axis runs over, the one named last changes fastest.
Arguments:
- vectors: float32 [2, 8, 262144], P('spin', None, 'dom'), may hold values from -17 to 17
- basis: float32 [2, 16, 262144], P('spin', None, 'dom'), may hold values from -17 to 17
- potential: float32 [2, 262144], P('spin', 'dom'), may hold values from 1 to 3
- hop_table: bfloat16 [8, 128, 128], replicated, may hold values from -0.25 to 0.25
- soc_table: bfloat16 [2, 128, 128], replicated, may hold values from -0.5 to 0.5
- nbr_block: int32 [2048, 16], P('dom'), may hold values from 0 to 2047, as said below
- nbr_type: int32 [2048, 16], P('dom'), may hold values from 0 to 7
- nbr_count: int32 [2048], P('dom'), may hold values from 1 to 16, as said below
- flip_block: int32 [2048], P('dom'), may hold values from 0 to 2047, as said below
Outputs:
- block_one: float32 [2, 8, 262144], P('spin', None, 'dom')
- block_two: float32 [2, 8, 262144], P('spin', None, 'dom')
- coefs_one: float32 [32, 8], replicated
- coefs_two: float32 [40, 8], replicated
Inputs may be any that keep to these rules, and one draw needn't show every extreme that they name: nbr_block[i, l] equals i + d modulo 2048 with -8 <= d <= 8; slots at or beyond nbr_count[i] are ignored; in slot 0, the first block of each group of 128 has d = -8 and the last has d = 8. `nbr_count`: some block has all 16 slots live. flip_block[i] lies in the same domain as i: flip_block[i] // 128 == i // 128.
All inputs are finite; a program needn't handle non-finite values.
Results may differ from a plain program's by a relative error of at most 0.0033.
Values may be sent and summed in bfloat16 or wider, within the bound.
A program may use at most 64 MiB of HBM per device.

v0:
```python
import jax
import jax.numpy as jnp
from jax import lax
from jax.sharding import PartitionSpec as P

RANGE = 8


def extended_2(cells, sides, width):
    for axis, dim in sides:
        count = lax.axis_size(axis)
        head = lax.slice_in_dim(cells, 0, width, axis=dim)
        tail = lax.slice_in_dim(cells, cells.shape[dim] - width, cells.shape[dim], axis=dim)
        cells = jnp.concatenate(
            [
                lax.ppermute(tail, axis, [(i, (i + 1) % count) for i in range(count)]),
                cells,
                lax.ppermute(head, axis, [((i + 1) % count, i) for i in range(count)]),
            ],
            axis=dim,
        )
    return cells


def partner(block, axis, distance):
    count = lax.axis_size(axis)
    route = []
    for low in range(count):
        high = low | 1 << distance
        if high != low and high < count:
            route += [(low, high), (high, low)]
    return lax.ppermute(block, axis, route)


def inner_rows(left_rows, right_rows):
    return lax.dot_general(
        left_rows, right_rows, (((1,), (1,)), ((), ())), precision=lax.Precision.HIGHEST
    )


def times_rows(coef_matrix, span_rows):
    return lax.dot_general(
        coef_matrix, span_rows, (((0,), (0,)), ((), ())), precision=lax.Precision.HIGHEST
    )


def small_product(left_matrix, right_matrix):
    return jnp.dot(left_matrix, right_matrix, precision=lax.Precision.HIGHEST)


def per_device(
    vectors, basis, potential, hop_table, soc_table, nbr_block, nbr_type, nbr_count, flip_block
):
    block_local = nbr_block.shape[0]
    block_width = hop_table.shape[1]
    type_total = hop_table.shape[0]
    slot_total = nbr_block.shape[1]
    vector_count = vectors.shape[1]
    domain_total = lax.axis_size("dom")
    block_total = block_local * domain_total
    norm_count = float(2 * block_local * block_width * domain_total)
    first_block = lax.axis_index("dom") * block_local
    spin_index = lax.axis_index("spin")
    local_index = jnp.arange(block_local, dtype=jnp.int32)
    offset = (nbr_block - (first_block + local_index)[:, None] + RANGE) % block_total - RANGE
    flat_index = (local_index[:, None] + RANGE + offset) * type_total + nbr_type
    live_mask = (jnp.arange(slot_total, dtype=jnp.int32)[None, :] < nbr_count[:, None]).astype(
        jnp.float32
    )
    flip_local = flip_block - first_block
    soc_own = lax.dynamic_index_in_dim(soc_table, spin_index, 0, keepdims=False)
    onsite = potential[0]

    def apply_operator(field):
        rounded = field.reshape(vector_count, block_local, block_width).astype(jnp.bfloat16)
        extended = extended_2(rounded, (("dom", 1),), RANGE)
        products = jnp.einsum(
            "kjc,tbc->kjtb", extended, hop_table, preferred_element_type=jnp.float32
        )
        products = products.reshape(vector_count, -1, block_width)
        gathered = jnp.take(products, flat_index.reshape(-1), axis=1)
        gathered = gathered.reshape(vector_count, block_local, slot_total, block_width)
        hopping = jnp.sum(gathered * live_mask[None, :, :, None], axis=2)
        other_side = partner(rounded, "spin", 0)
        picked = jnp.take(other_side, flip_local, axis=1)
        flip_term = jnp.einsum("kic,bc->kib", picked, soc_own, preferred_element_type=jnp.float32)
        return onsite[None, :] * field + (hopping + flip_term).reshape(vector_count, -1)

    def orthonormal(span, image):
        span_gram, correlation, image_gram = lax.psum(
            (inner_rows(span, span), inner_rows(span, image), inner_rows(image, image)),
            ("dom", "spin"),
        )
        span_gram = span_gram / norm_count
        first_coef = correlation / norm_count
        image_gram = image_gram / norm_count
        total_coef = 2.0 * first_coef - small_product(span_gram, first_coef)
        twice = image - times_rows(total_coef, span)
        gram_matrix = (
            image_gram
            - small_product(total_coef.T, first_coef)
            - small_product(first_coef.T, total_coef)
            + small_product(total_coef.T, small_product(span_gram, total_coef))
        )
        lower_factor = jnp.linalg.cholesky(gram_matrix)
        new_block = lax.linalg.triangular_solve(lower_factor, twice, left_side=True, lower=True)
        coefs = jnp.concatenate([total_coef, lower_factor.T], axis=0)
        return (new_block, coefs)

    current = vectors[0]
    span = jnp.concatenate([basis[0], current], axis=0)
    block_one, coefs_one = orthonormal(span, apply_operator(current))
    span_two = jnp.concatenate([span, block_one], axis=0)
    block_two, coefs_two = orthonormal(span_two, apply_operator(block_one))
    return (block_one[None], block_two[None], coefs_one, coefs_two)


def solution(mesh):
    return jax.shard_map(
        per_device,
        mesh=mesh,
        in_specs=(
            P("spin", None, "dom"),
            P("spin", None, "dom"),
            P("spin", "dom"),
            P(),
            P(),
            P("dom", None),
            P("dom", None),
            P("dom"),
            P("dom"),
        ),
        out_specs=(P("spin", None, "dom"), P("spin", None, "dom"), P(), P()),
        check_vma=False,
    )
```

profile of v0, /device:TPU:0, one launch (start us, length us, event | category | flops | bytes accessed | tf_op | source)
XLA Modules:
  0.0 202.6 jit_solution(12468295660769314962)
XLA Ops:
  0.6 1.2 copy.121
  1.8 0.6 collective-permute-start.2
  2.4 2.5 %collective-permute-start = (bf16[8,8,128]{2,1,0:T(8,128)(2,1)S(1)}, bf16[8,8,128]{2,1,0:T(8,128)(2,1)S(1)}, u32[]{:S(2)}, u32[]{:S(2)}) collective-permute-start(bf16[8,8,128]{2,1,0:T(8,128)(2,1)S(1)} %get-tuple-element.18), channel_id=1, source_target_pairs={{0,2},{2,4},{4,6},{6,8},{8,10},{10,12},{12,14},{14,16},{16,18},{18... | collective-permute-start | bytes 49160 | tf_op jit(solution)/shard_map/ppermute | solution.py:16
  5.0 4.1 %collective-permute-start.1 = (bf16[8,8,128]{2,1,0:T(8,128)(2,1)S(1)}, bf16[8,8,128]{2,1,0:T(8,128)(2,1)S(1)}, u32[]{:S(2)}, u32[]{:S(2)}) collective-permute-start(bf16[8,8,128]{2,1,0:T(8,128)(2,1)S(1)} %get-tuple-element.19), channel_id=1, source_target_pairs={{2,0},{4,2},{6,4},{8,6},{10,8},{12,10},{14,12},{16,14},{18,16},{20... | collective-permute-start | bytes 49160 | tf_op jit(solution)/shard_map/ppermute | solution.py:18
  9.0 0.7 fusion.40
  9.7 0.1 copy.55
  9.8 0.1 reshape.99
  10.0 0.7 fusion.25
  10.7 1.2 compare_and_fusion.1
  11.9 4.2 %fusion.1 = f32[24,24]{1,0:T(8,128)} fusion(f32[8,16384]{1,0:T(8,128)} %bitcast.113, f32[16,16384]{1,0:T(8,128)} %bitcast.122), kind=kOutput, calls=%fused_computation.27 | convolution fusion | flops 113639424 | bytes 1575168 | tf_op jit(solution)/shard_map/dot_general | solution.py:36
  16.1 0.8 fusion.8
  16.8 1.4 copy.120
  18.3 7.5 %copy.57 = f32[8,1152,128]{2,0,1:T(8,128)} copy(f32[8,1152,128]{2,1,0:T(8,128)S(1)} %bitcast.120) | data formatting | bytes 9437184 | tf_op jit(solution)/shard_map/reshape | solution.py:80
  25.8 18.1 %gather_fusion = f32[2048,8,128]{2,1,0:T(8,128)} fusion(f32[8,1152,128]{2,0,1:T(8,128)} %copy.57, s32[2048]{0:T(1024)S(1)} %fusion.43), kind=kCustom, calls=%fused_computation.clone | custom fusion | bytes 16785408 | tf_op jit(solution)/shard_map/jit(_take)/gather | solution.py:81
  43.9 9.2 %multiply_reduce_fusion.1 = f32[8,128,128]{2,0,1:T(8,128)S(1)} fusion(f32[128,16]{1,0:T(8,128)S(1)} %fusion.25, f32[2048,8,128]{2,1,0:T(8,128)} %gather_fusion, pred[2048]{0:T(1024)(128)(4,1)S(1)} %compare_and_fusion), kind=kLoop, calls=%fused_computation.8 | loop fusion | flops 6160384 | bytes 8923136 | tf_op jit(solution)/shard_map/reduce_sum | solution.py:83
  53.1 0.2 copy.58
  53.3 0.7 gather_fusion.1
  54.0 0.9 select_bitcast_fusion.1
  54.9 1.1 fusion.5
  56.0 1.3 convolution_bitcast_fusion.1
  57.3 1.6 fusion.2
  59.0 38.1 %all-reduce.1 = (f32[24,24]{1,0:T(8,128)S(1)}, f32[24,8]{0,1:T(8,128)S(1)}, f32[8,8]{0,1:T(8,128)S(1)}) all-reduce(f32[24,24]{1,0:T(8,128)S(1)} %copy-done.5, f32[24,8]{0,1:T(8,128)S(1)} %fusion.2, f32[8,8]{0,1:T(8,128)S(1)} %convolution_bitcast_fusion.1), channel_id=1, replica_groups=mesh['dom'=16,'spin'=2] {'dom','spin'}, use_global_device_ids=true, to_apply=%region_3.6 | all-reduce | flops 832 | bytes 6656 | tf_op jit(solution)/shard_map/psum | solution.py:90
  97.1 0.1 convolution_subtract_fusion.7
  97.2 0.1 fusion.33
  97.3 1.2 convolution_subtract_fusion.1
  98.5 0.1 convolution_subtract_fusion.6
  98.6 0.1 convolution_subtract_fusion.5
  98.8 0.1 convolution_add_fusion.3
  98.9 0.1 copy.67
  99.0 0.7 cholesky.44
  99.8 0.6 compare_reduce_fusion.1
  100.4 0.6 fusion.58
  101.1 0.6 custom-call.6
  101.7 0.6 fusion.47
  102.4 0.1 collective-permute-start.5
  102.5 2.4 %fusion.3 = f32[32,32]{1,0:T(8,128)} fusion(f32[8,16384]{1,0:T(8,128)S(1)} %fusion.47, f32[8,16384]{1,0:T(8,128)S(1)} %bitcast.117, f32[16,16384]{1,0:T(8,128)S(1)} %bitcast.125), kind=kOutput, calls=%fused_computation.29 | convolution fusion | flops 202375168 | bytes 2101248 | tf_op jit(solution)/shard_map/dot_general | solution.py:36
  104.9 2.3 %collective-permute-start.3 = (bf16[8,8,128]{2,1,0:T(8,128)(2,1)S(1)}, bf16[8,8,128]{2,1,0:T(8,128)(2,1)S(1)}, u32[]{:S(2)}, u32[]{:S(2)}) collective-permute-start(bf16[8,8,128]{2,1,0:T(8,128)(2,1)S(1)} %get-tuple-element.16), channel_id=1, source_target_pairs={{0,2},{2,4},{4,6},{6,8},{8,10},{10,12},{12,14},{14,16},{16,18},{18... | collective-permute-start | bytes 49160 | tf_op jit(solution)/shard_map/ppermute | solution.py:16
  107.2 3.3 %collective-permute-start.4 = (bf16[8,8,128]{2,1,0:T(8,128)(2,1)S(1)}, bf16[8,8,128]{2,1,0:T(8,128)(2,1)S(1)}, u32[]{:S(2)}, u32[]{:S(2)}) collective-permute-start(bf16[8,8,128]{2,1,0:T(8,128)(2,1)S(1)} %get-tuple-element.17), channel_id=1, source_target_pairs={{2,0},{4,2},{6,4},{8,6},{10,8},{12,10},{14,12},{16,14},{18,16},{20... | collective-permute-start | bytes 49160 | tf_op jit(solution)/shard_map/ppermute | solution.py:18
  110.5 0.7 pad_maximum_fusion.8
  111.2 1.0 collective-permute-done.3
  112.2 0.8 fusion.13
  113.0 1.4 copy.119
  114.4 7.5 %copy.73 = f32[8,1152,128]{2,0,1:T(8,128)} copy(f32[8,1152,128]{2,1,0:T(8,128)S(1)} %bitcast.121) | data formatting | bytes 9437184 | tf_op jit(solution)/shard_map/reshape | solution.py:80
  122.0 18.1 %gather_fusion.2 = f32[2048,8,128]{2,1,0:T(8,128)} fusion(f32[8,1152,128]{2,0,1:T(8,128)} %copy.73, s32[2048]{0:T(1024)S(1)} %fusion.43), kind=kCustom, calls=%fused_computation.2.clone | custom fusion | bytes 16785408 | tf_op jit(solution)/shard_map/jit(_take)/gather | solution.py:81
  140.1 9.1 %multiply_reduce_fusion = f32[8,128,128]{2,0,1:T(8,128)S(1)} fusion(f32[128,16]{1,0:T(8,128)S(1)} %fusion.25, f32[2048,8,128]{2,1,0:T(8,128)} %gather_fusion.2, pred[2048]{0:T(1024)(128)(4,1)S(1)} %compare_and_fusion), kind=kLoop, calls=%fused_computation.7 | loop fusion | flops 6160384 | bytes 8923136 | tf_op jit(solution)/shard_map/reduce_sum | solution.py:83
  149.2 1.6 gather_fusion.3
  150.9 0.2 select_bitcast_fusion
  151.1 1.0 fusion
  152.1 1.3 fusion.7
  153.4 1.9 fusion.4
  155.3 40.4 %all-reduce = (f32[32,32]{1,0:T(8,128)S(1)}, f32[32,8]{0,1:T(8,128)S(1)}, f32[8,8]{0,1:T(8,128)S(1)}) all-reduce(f32[32,32]{1,0:T(8,128)S(1)} %copy-done.6, f32[32,8]{0,1:T(8,128)S(1)} %fusion.4, f32[8,8]{0,1:T(8,128)S(1)} %fusion.7), channel_id=1, replica_groups=mesh['dom'=16,'spin'=2] {'dom','spin'}, use_global_device_ids=true, to_apply=%region_9.14 | all-reduce | flops 1344 | bytes 10752 | tf_op jit(solution)/shard_map/psum | solution.py:90
  195.7 0.1 convolution_subtract_fusion.4
  195.8 0.1 fusion.30
  196.0 1.3 convolution_subtract_fusion
  197.3 0.1 convolution_subtract_fusion.3
  197.4 0.1 convolution_subtract_fusion.2
  197.6 0.1 convolution_add_fusion.2
  197.7 0.1 copy.80
  197.8 0.7 cholesky.55
  198.6 0.6 compare_reduce_fusion
  199.2 0.6 fusion.59
  199.9 0.7 pad_maximum_fusion.9
  200.5 0.6 custom-call.7
  201.2 1.4 convolution_bitcast_fusion
  (33 shorter events, 0.3 us)
Async XLA Ops:
  0.6 15.4 %copy-start = (bf16[8,128,128]{2,1,0:T(8,128)(2,1)S(1)}, bf16[8,128,128]{2,1,0:T(8,128)(2,1)}, u32[]{:S(2)}) copy-start(bf16[8,128,128]{2,1,0:T(8,128)(2,1)} %param.19) | copy-start | bytes 786436
  1.8 51.3 %collective-permute-start.2 = (bf16[8,128,128]{2,1,0:T(8,128)(2,1)S(1)}, bf16[8,128,128]{2,1,0:T(8,128)(2,1)S(1)}, u32[]{:S(2)}, u32[]{:S(2)}) collective-permute-start(bf16[8,128,128]{2,1,0:T(8,128)(2,1)S(1)} %bitcast.137), channel_id=1, source_target_pairs={{0,1},{1,0},{2,3},{3,2},{4,5},{5,4},{6,7},{7,6},{8,9},{9,8},{10,11... | collective-permute-start | bytes 786440 | tf_op jit(solution)/shard_map/ppermute | solution.py:32
  2.4 13.6 %collective-permute-start = (bf16[8,8,128]{2,1,0:T(8,128)(2,1)S(1)}, bf16[8,8,128]{2,1,0:T(8,128)(2,1)S(1)}, u32[]{:S(2)}, u32[]{:S(2)}) collective-permute-start(bf16[8,8,128]{2,1,0:T(8,128)(2,1)S(1)} %get-tuple-element.18), channel_id=1, source_target_pairs={{0,2},{2,4},{4,6},{6,8},{8,10},{10,12},{12,14},{14,16},{16,18},{18... | collective-permute-start | bytes 49160 | tf_op jit(solution)/shard_map/ppermute | solution.py:16
  5.0 11.1 %collective-permute-start.1 = (bf16[8,8,128]{2,1,0:T(8,128)(2,1)S(1)}, bf16[8,8,128]{2,1,0:T(8,128)(2,1)S(1)}, u32[]{:S(2)}, u32[]{:S(2)}) collective-permute-start(bf16[8,8,128]{2,1,0:T(8,128)(2,1)S(1)} %get-tuple-element.19), channel_id=1, source_target_pairs={{2,0},{4,2},{6,4},{8,6},{10,8},{12,10},{14,12},{16,14},{18,16},{20... | collective-permute-start | bytes 49160 | tf_op jit(solution)/shard_map/ppermute | solution.py:18
  43.9 11.0 %copy-start.1 = (f32[1,8,16384]{2,1,0:T(8,128)S(1)}, f32[1,8,16384]{2,1,0:T(8,128)}, u32[]{:S(2)}) copy-start(f32[1,8,16384]{2,1,0:T(8,128)} %param.16) | copy-start | bytes 1572868
  43.9 11.0 %copy-start.4 = (f32[1,16384]{1,0:T(1,128)S(1)}, f32[1,16384]{1,0:T(1,128)}, u32[]{:S(2)}) copy-start(f32[1,16384]{1,0:T(1,128)} %param.18) | copy-start | bytes 196612
  53.3 4.0 %copy-start.2 = (f32[1,16,16384]{2,1,0:T(8,128)S(1)}, f32[1,16,16384]{2,1,0:T(8,128)}, u32[]{:S(2)}) copy-start(f32[1,16,16384]{2,1,0:T(8,128)} %param.17) | copy-start | bytes 3145732
  54.9 4.0 %copy-start.5 = (f32[24,24]{1,0:T(8,128)S(1)}, f32[24,24]{1,0:T(8,128)}, u32[]{:S(2)}) copy-start(f32[24,24]{1,0:T(8,128)} %fusion.1) | copy-start | bytes 6916
  102.3 93.7 %copy-start.3 = (f32[8,16384]{1,0:T(8,128)}, f32[8,16384]{1,0:T(8,128)S(1)}, u32[]{:S(2)}) copy-start(f32[8,16384]{1,0:T(8,128)S(1)} %fusion.47) | copy-start | bytes 1572868
  102.4 46.8 %collective-permute-start.5 = (bf16[8,128,128]{2,0,1:T(8,128)(2,1)S(1)}, bf16[8,128,128]{2,0,1:T(8,128)(2,1)}, u32[]{:S(2)}, u32[]{:S(2)}) collective-permute-start(bf16[8,128,128]{2,0,1:T(8,128)(2,1)S(1)} %convert_bitcast_fusion), channel_id=1, source_target_pairs={{0,1},{1,0},{2,3},{3,2},{4,5},{5,4},{6,7},{7,6},{8,9},{9,8},{10,11... | collective-permute-start | bytes 786440 | tf_op jit(solution)/shard_map/ppermute | solution.py:32
  104.9 7.3 %collective-permute-start.3 = (bf16[8,8,128]{2,1,0:T(8,128)(2,1)S(1)}, bf16[8,8,128]{2,1,0:T(8,128)(2,1)S(1)}, u32[]{:S(2)}, u32[]{:S(2)}) collective-permute-start(bf16[8,8,128]{2,1,0:T(8,128)(2,1)S(1)} %get-tuple-element.16), channel_id=1, source_target_pairs={{0,2},{2,4},{4,6},{6,8},{8,10},{10,12},{12,14},{14,16},{16,18},{18... | collective-permute-start | bytes 49160 | tf_op jit(solution)/shard_map/ppermute | solution.py:16
  107.2 5.1 %collective-permute-start.4 = (bf16[8,8,128]{2,1,0:T(8,128)(2,1)S(1)}, bf16[8,8,128]{2,1,0:T(8,128)(2,1)S(1)}, u32[]{:S(2)}, u32[]{:S(2)}) collective-permute-start(bf16[8,8,128]{2,1,0:T(8,128)(2,1)S(1)} %get-tuple-element.17), channel_id=1, source_target_pairs={{2,0},{4,2},{6,4},{8,6},{10,8},{12,10},{14,12},{16,14},{18,16},{20... | collective-permute-start | bytes 49160 | tf_op jit(solution)/shard_map/ppermute | solution.py:18
  140.1 10.8 %copy-start.7 = (pred[128]{0:T(512)(128)(4,1)S(1)}, pred[128]{0:T(512)(128)(4,1)}, u32[]{:S(2)}) copy-start(pred[128]{0:T(512)(128)(4,1)} %get-tuple-element.14) | copy-start | bytes 388
  152.1 3.2 %copy-start.6 = (f32[32,32]{1,0:T(8,128)S(1)}, f32[32,32]{1,0:T(8,128)}, u32[]{:S(2)}) copy-start(f32[32,32]{1,0:T(8,128)} %fusion.3) | copy-start | bytes 12292
where the time goes:
time: 203 us
  blocking collectives  78.5 us (39%)
  local copies, waits for them, and re-layouts  58.3 us (29%)
  other arithmetic  28.8 us (14%)
  matrix products  22.2 us (11%)
  starting transfers between devices  12.9 us (6%)
    psum x2, blocking collectives, orthonormal(): lax.psum((inner_rows(span, span), inner_rows(span, image), inner_rows(ima...  78.5 us
    gather x2, local copies, waits for them, and re-layouts, apply_operator(): gathered = jnp.take(products, flat_index.reshape(-1), axis=1)  36.3 us
    reduce_sum x2, other arithmetic, apply_operator(): hopping = jnp.sum(gathered * live_mask[None, :, :, None], axis=2)  18.3 us
    reshape x2, local copies, waits for them, and re-layouts, apply_operator(): products = products.reshape(vector_count, -1, block_width)  15.1 us
    dot_general x6, matrix products, inner_rows(): lax.dot_general(left_rows, right_rows, (((1,), (1,)), ((), ())), precisio...  12.6 us
    ppermute x2, starting transfers between devices, extended_2(): lax.ppermute(head, axis, [((i + 1) % count, i) for i in range(count)])  7.41 us
    ppermute x2, starting transfers between devices, extended_2(): lax.ppermute(tail, axis, [(i, (i + 1) % count) for i in range(count)])  4.82 us
  transfers between devices with their start and end apart: 6, of which 1 were waited for; matrix products, arithmetic and copies ran while one was open for 42% of the time, Pallas kernels for 0%

commit v1 on v0

v1 whole, which is shorter than its diff:
```python
import functools
import jax
import jax.numpy as jnp
from jax import lax
from jax.experimental import pallas as pl
from jax.experimental.pallas import tpu as pltpu
from jax.sharding import PartitionSpec as P

RANGE = 8
MESH = pl.DeviceIdType.MESH
NT = (((1,), (1,)), ((), ()))
NN = (((1,), (0,)), ((), ()))


def high_dot(left, right, dims):
    return lax.dot_general(
        left, right, dims, precision=lax.Precision.HIGHEST, preferred_element_type=jnp.float32
    )


def kernel(
    cfg,
    vec_ref, basis_ref, pot_ref, hop_ref, soc_ref, idx_ref,
    one_ref, two_ref, coef_one_ref, coef_two_ref,
    ext_ref, other_ref, halo_ref, prod_ref, image_ref, bcast_ref, stage_a_ref, stage_b_ref,
    link_send, link_recv, a_send, a_recv, b_send, b_recv,
):
    dom_total, group_doms, blocks, width, types, slots, vecs, kept, norm = cfg
    groups = dom_total // group_doms
    group_size = 2 * group_doms
    dom, spin = lax.axis_index("dom"), lax.axis_index("spin")
    rank_a = (dom % group_doms) * 2 + spin
    rank_b = dom // group_doms
    dom_base = rank_b * group_doms
    left, right = (dom + dom_total - 1) % dom_total, (dom + 1) % dom_total
    rows = blocks * vecs
    halo_rows = RANGE * vecs
    reach = blocks + 2 * RANGE
    zero_tile = reach * types
    flip_base = zero_tile + 1

    def peer_a(shift):
        other = (rank_a + shift) % group_size
        return (dom_base + other // 2, other % 2)

    def peer_b(shift):
        return (((rank_b + shift) % groups) * group_doms + dom % group_doms, spin)

    barrier = pltpu.get_barrier_semaphore()
    for shift in range(1, group_size):
        pl.semaphore_signal(barrier, inc=1, device_id=peer_a(shift), device_id_type=MESH)
    for shift in range(1, groups):
        pl.semaphore_signal(barrier, inc=1, device_id=peer_b(shift), device_id_type=MESH)
    for side in (left, right):
        pl.semaphore_signal(barrier, inc=1, device_id=(side, spin), device_id_type=MESH)

    lane = lax.broadcasted_iota(jnp.int32, (vecs, width), 1)
    row = lax.broadcasted_iota(jnp.int32, (vecs, width), 0)

    def cols(tile):
        return pl.ds(pl.multiple_of(tile * width, width), width)

    def link_copies(app):
        ext, halo = ext_ref.at[app], halo_ref.at[app]
        tail = pltpu.make_async_remote_copy(
            src_ref=ext.at[pl.ds(rows - halo_rows, halo_rows)],
            dst_ref=halo.at[pl.ds(0, halo_rows)],
            send_sem=link_send.at[app, 0], recv_sem=link_recv.at[app, 0],
            device_id=(right, spin), device_id_type=MESH)
        head = pltpu.make_async_remote_copy(
            src_ref=ext.at[pl.ds(0, halo_rows)],
            dst_ref=halo.at[pl.ds(halo_rows, halo_rows)],
            send_sem=link_send.at[app, 1], recv_sem=link_recv.at[app, 1],
            device_id=(left, spin), device_id_type=MESH)
        flip = pltpu.make_async_remote_copy(
            src_ref=ext, dst_ref=other_ref.at[app],
            send_sem=link_send.at[app, 2], recv_sem=link_recv.at[app, 2],
            device_id=(dom, 1 - spin), device_id_type=MESH)
        return tail, head, flip

    def gram_rows(left_ref, sources):
        count = sum(hi for _, hi in sources)

        def body(tile, sums):
            ours = left_ref[:, cols(tile)]
            picked = [ref[pl.ds(m, 1), cols(tile)] for ref, hi in sources for m in range(hi)]
            return tuple(total + ours * one for total, one in zip(sums, picked))

        sums = lax.fori_loop(
            0, blocks, body, tuple(jnp.zeros((vecs, width), jnp.float32) for _ in range(count)),
            unroll=2)
        out = jnp.zeros((vecs, width), jnp.float32)
        for m, total in enumerate(sums):
            out = jnp.where(lane == m, jnp.sum(total, axis=1, keepdims=True), out)
        return out

    def products(source, count, first):
        def body(pair, carry):
            weights = hop_ref[pl.ds(pl.multiple_of(pair * 2 * width, 2 * width), 2 * width), :]
            out = lax.dot_general(source[...], weights, NT, preferred_element_type=jnp.float32)
            for half in range(2):
                part = out[:, half * width:(half + 1) * width].reshape(count, vecs, width)
                prod_ref[pl.ds((pair * 2 + half) * reach + first, count)] = part
            return carry
        lax.fori_loop(0, types // 2, body, 0)

    def flip_products(app):
        out = lax.dot_general(
            other_ref[app], soc_ref[spin], NT, preferred_element_type=jnp.float32)
        prod_ref[pl.ds(flip_base, blocks)] = out.reshape(blocks, vecs, width)

    def gather(field_ref, low, high):
        def body(block, carry):
            terms = [pot_ref[pl.ds(0, 1), cols(block)] * field_ref[:, cols(block)]]
            for slot in range(slots + 1):
                terms.append(prod_ref[idx_ref[block * (slots + 1) + slot]])
            while len(terms) > 1:
                terms = [sum(terms[p:p + 2][1:], terms[p]) for p in range(0, len(terms), 2)]
            image_ref[:, cols(block)] = terms[0]
            return carry
        lax.fori_loop(low, high, body, 0, unroll=2)

    def share(app, value):
        def stage(ref, send, recv, rank, size, peer, mine):
            ref[app, rank] = mine
            def copy(shift, slot):
                return pltpu.make_async_remote_copy(
                    src_ref=ref.at[app, rank], dst_ref=ref.at[app, slot],
                    send_sem=send.at[app, shift], recv_sem=recv.at[app, slot],
                    device_id=peer(shift), device_id_type=MESH)
            for shift in range(1, size):
                copy(shift, rank).start()
            for shift in range(1, size):
                copy(shift, (rank + size - shift) % size).wait_recv()
            for shift in range(1, size):
                copy(shift, rank).wait_send()
            total = ref[app, 0]
            for slot in range(1, size):
                total = total + ref[app, slot]
            return total
        value = stage(stage_a_ref, a_send, a_recv, rank_a, group_size, peer_a, value)
        if groups > 1:
            value = stage(stage_b_ref, b_send, b_recv, rank_b, groups, peer_b, value)
        return value * (1.0 / norm)

    def lanes(value, start, count):
        moved = value if start == 0 else pltpu.roll(value, width - start, 1)
        return jnp.where(lane < count, moved, 0.0)

    def tall(pieces):
        pad = width - vecs * len(pieces)
        return jnp.concatenate(list(pieces) + [jnp.zeros((pad, width), jnp.float32)], axis=0)

    def factor(first_t, image_gram, span_gram, span_count):
        total_t = 2.0 * first_t - high_dot(first_t, span_gram, NT)
        moved = high_dot(total_t, span_gram, NT) - first_t
        gram = image_gram + high_dot(moved, tall([total_t]), NT) - high_dot(total_t, tall([first_t]), NT)
        table = jnp.where(lane < vecs, gram, jnp.where(lane == row + vecs, 1.0, 0.0))
        table = table - pltpu.roll(total_t, 2 * vecs, 1)
        for j in range(vecs):
            column = jnp.broadcast_to(table[:, j:j + 1], (vecs, width))
            pivot_row = jnp.broadcast_to(table[j:j + 1, :], (vecs, width))
            pivot = jnp.broadcast_to(column[j:j + 1, :], (vecs, width))
            scale = 1.0 / jnp.sqrt(pivot)
            pivot_row = pivot_row * scale
            table = jnp.where(
                row == j, pivot_row, jnp.where(row > j, table - column * scale * pivot_row, table))
        upper = jnp.where((lane >= row) & (lane < vecs), table, 0.0)
        for m in range(vecs + span_count):
            bcast_ref[m] = jnp.broadcast_to(table[:, vecs + m:vecs + m + 1], (vecs, width))
        return total_t + pltpu.roll(upper, 64, 1)

    def combine(sources, out_ref, ext_out):
        step = 4

        def body(chunk, carry):
            sums = [None] * step
            m = 0
            for ref, hi in sources:
                for r in range(hi):
                    coef = bcast_ref[m]
                    for u in range(step):
                        term = coef * ref[pl.ds(r, 1), cols(chunk * step + u)]
                        sums[u] = term if sums[u] is None else sums[u] + term
                    m += 1
            for u in range(step):
                out_ref[:, cols(chunk * step + u)] = sums[u]
            if ext_out is not None:
                for u in range(0, step, 2):
                    pair = jnp.concatenate(sums[u:u + 2], axis=0).astype(jnp.bfloat16)
                    at = pl.multiple_of((chunk * step + u) * vecs, 2 * vecs)
                    ext_out[pl.ds(at, 2 * vecs), :] = pair
            return carry
        return step, body

    field, basis = vec_ref.at[0], basis_ref.at[0]
    one, two = one_ref.at[0], two_ref.at[0]

    def round_body(pair, carry):
        both = jnp.concatenate([field[:, cols(2 * pair)], field[:, cols(2 * pair + 1)]], axis=0)
        ext_ref[0, pl.ds(pl.multiple_of(pair * 2 * vecs, 2 * vecs), 2 * vecs), :] = both.astype(
            jnp.bfloat16)
        return carry

    lax.fori_loop(0, blocks // 2, round_body, 0, unroll=4)
    prod_ref[zero_tile] = jnp.zeros((vecs, width), jnp.float32)
    low_gram = [gram_rows(basis.at[pl.ds(g * vecs, vecs)], [(basis, (g + 1) * vecs)])
                for g in range(kept // vecs)]
    low_gram.append(gram_rows(field, [(basis, kept), (field, vecs)]))
    pl.semaphore_wait(barrier, group_size - 1 + groups - 1 + 2)

    def apply_and_gram(app, field_ref, extra, sources):
        tail, head, flip = link_copies(app)
        products(ext_ref.at[app], blocks, 0)
        early = extra()
        flip.wait_recv()
        flip_products(app)
        gather(field_ref, RANGE, blocks - RANGE)
        tail.wait_recv()
        head.wait_recv()
        products(halo_ref.at[app], 2 * RANGE, blocks)
        gather(field_ref, 0, RANGE)
        gather(field_ref, blocks - RANGE, blocks)
        result = gram_rows(image_ref, sources + [(image_ref, vecs)])
        tail.wait_send()
        head.wait_send()
        flip.wait_send()
        return result, early

    for copy in link_copies(0):
        copy.start()
    span_one = kept + vecs
    result, _ = apply_and_gram(0, field, lambda: None, [(basis, kept), (field, vecs)])
    packed = result
    at = span_one + vecs
    for g in range(span_one // vecs):
        packed = packed + pltpu.roll(low_gram[g], at, 1)
        at += (g + 1) * vecs
    packed = share(0, packed)
    pieces = []
    at = span_one + vecs
    for g in range(span_one // vecs):
        pieces.append(lanes(packed, at, (g + 1) * vecs))
        at += (g + 1) * vecs
    low = tall(pieces)
    wide_row = lax.broadcasted_iota(jnp.int32, (width, width), 0) // vecs
    wide_lane = lax.broadcasted_iota(jnp.int32, (width, width), 1) // vecs
    span_gram = low + jnp.where(wide_row < wide_lane, low.T, 0.0)
    coef_one_ref[...] = factor(
        lanes(packed, 0, span_one), lanes(packed, span_one, vecs), span_gram, span_one)

    step, body = combine([(image_ref, vecs), (basis, kept), (field, vecs)], one, ext_ref.at[1])
    chunks, edge = blocks // step, RANGE // step
    tail, head, flip = link_copies(1)
    lax.fori_loop(0, edge, body, 0)
    lax.fori_loop(chunks - edge, chunks, body, 0)
    tail.start()
    head.start()
    lax.fori_loop(edge, chunks - edge, body, 0)
    flip.start()

    span_two = span_one + vecs
    result, early = apply_and_gram(
        1, one,
        lambda: gram_rows(one, [(basis, kept), (field, vecs), (one, vecs)]),
        [(basis, kept), (field, vecs), (one, vecs)])
    packed = share(1, result + pltpu.roll(early, 64, 1))
    low = jnp.concatenate(
        [jnp.zeros((span_one, width), jnp.float32), lanes(packed, 64, span_two),
         jnp.zeros((width - span_two, width), jnp.float32)], axis=0)
    span_gram = span_gram + low + jnp.where(wide_row < wide_lane, low.T, 0.0)
    coef_two_ref[...] = factor(
        lanes(packed, 0, span_two), lanes(packed, span_two, vecs), span_gram, span_two)
    step, body = combine(
        [(image_ref, vecs), (basis, kept), (field, vecs), (one, vecs)], two, None)
    lax.fori_loop(0, chunks, body, 0)


def per_device(
    vectors, basis, potential, hop_table, soc_table, nbr_block, nbr_type, nbr_count, flip_block
):
    blocks, slots = nbr_block.shape
    types, width, _ = hop_table.shape
    vecs, kept = vectors.shape[1], basis.shape[1]
    dom_total = lax.axis_size("dom")
    group_doms = 4 if dom_total % 4 == 0 else 1
    groups = dom_total // group_doms
    block_total = blocks * dom_total
    reach = blocks + 2 * RANGE
    norm = float(2 * blocks * width * dom_total)
    first_block = lax.axis_index("dom") * blocks
    local = jnp.arange(blocks, dtype=jnp.int32)
    offset = (nbr_block - (first_block + local)[:, None] + RANGE) % block_total - RANGE
    place = local[:, None] + offset
    place = jnp.where(
        place < 0, place + blocks + RANGE, jnp.where(place >= blocks, place + RANGE, place))
    live = jnp.arange(slots, dtype=jnp.int32)[None, :] < nbr_count[:, None]
    index = jnp.where(live, nbr_type * reach + place, reach * types)
    index = jnp.concatenate(
        [index, (flip_block - first_block + reach * types + 1)[:, None]], axis=1).reshape(-1)
    cfg = (dom_total, group_doms, blocks, width, types, slots, vecs, kept, norm)
    count = blocks * width
    rows = blocks * vecs
    vmem = pl.BlockSpec(memory_space=pltpu.VMEM)
    f32, bf16 = jnp.float32, jnp.bfloat16
    dma = pltpu.SemaphoreType.DMA
    one, two, coef_one, coef_two = pl.pallas_call(
        functools.partial(kernel, cfg),
        name="krylov",
        out_shape=(
            jax.ShapeDtypeStruct((1, vecs, count), f32),
            jax.ShapeDtypeStruct((1, vecs, count), f32),
            jax.ShapeDtypeStruct((vecs, width), f32),
            jax.ShapeDtypeStruct((vecs, width), f32),
        ),
        in_specs=[vmem] * 5 + [pl.BlockSpec(memory_space=pltpu.SMEM)],
        out_specs=(vmem,) * 4,
        scratch_shapes=[
            pltpu.VMEM((2, rows, width), bf16),
            pltpu.VMEM((2, rows, width), bf16),
            pltpu.VMEM((2, 2 * RANGE * vecs, width), bf16),
            pltpu.VMEM((reach * types + 1 + blocks, vecs, width), f32),
            pltpu.VMEM((vecs, count), f32),
            pltpu.VMEM((kept + 3 * vecs, vecs, width), f32),
            pltpu.VMEM((2, 2 * group_doms, vecs, width), f32),
            pltpu.VMEM((2, groups, vecs, width), f32),
            dma((2, 3)), dma((2, 3)),
            dma((2, 2 * group_doms)), dma((2, 2 * group_doms)),
            dma((2, groups)), dma((2, groups)),
        ],
        compiler_params=pltpu.CompilerParams(
            collective_id=0, has_side_effects=True, vmem_limit_bytes=48 * 1024 * 1024),
    )(vectors, basis, potential, hop_table.reshape(types * width, width), soc_table, index)

    def unpacked(tile, span_count):
        return jnp.concatenate([tile[:, :span_count].T, tile[:, 64:64 + vecs]], axis=0)

    return one, two, unpacked(coef_one, kept + vecs), unpacked(coef_two, kept + 2 * vecs)


def solution(mesh):
    return jax.shard_map(
        per_device,
        mesh=mesh,
        in_specs=(
            P("spin", None, "dom"),
            P("spin", None, "dom"),
            P("spin", "dom"),
            P(),
            P(),
            P("dom", None),
            P("dom", None),
            P("dom"),
            P("dom"),
        ),
        out_specs=(P("spin", None, "dom"), P("spin", None, "dom"), P(), P()),
        check_vma=False,
    )
```

time: 203 us -> 57.4 us (0.28)
  blocking collectives: 78.5 us -> 0 us
  local copies, waits for them, and re-layouts: 58.3 us -> 7.24 us
  Pallas kernels: 0 us -> 47 us
  other arithmetic: 28.8 us -> 2.06 us
  matrix products: 22.2 us -> 0 us
  starting transfers between devices: 12.9 us -> 0 us
    psum x2 -> x0, blocking collectives: 78.5 us -> none  [orthonormal(): lax.psum((inner_rows(span, span), inner_rows(span, image), inner_rows(ima...]
    pallas_call x0 -> x1, Pallas kernels: none -> 47 us  [per_device(): pl.pallas_call(functools.partial(kernel, cfg), name='krylov', out_shape=(...]
    gather x4 -> x0, local copies, waits for them, and re-layouts: 38.6 us -> none  [the longest x2 36.3 us: apply_operator(): gathered = jnp.take(products, flat_index.reshape(-1), axis=1)]
    dot_general x22 -> x0, matrix products: 20.1 us -> none  [the longest x6 12.6 us: inner_rows(): lax.dot_general(left_rows, right_rows, (((1,), (1,)), ((), ())), precisio...]
    reduce_sum x2 -> x0, other arithmetic: 18.3 us -> none  [apply_operator(): hopping = jnp.sum(gathered * live_mask[None, :, :, None], axis=2)]
    reshape x3 -> x1, local copies, waits for them, and re-layouts: 15.2 us -> 0.2 us  [per_device(): index = jnp.concatenate([index, (flip_block - first_block + reach * types...]
    ppermute x6 -> x0, starting transfers between devices: 12.9 us -> none  [the longest x2 7.41 us: extended_2(): lax.ppermute(head, axis, [((i + 1) % count, i) for i in range(count)])]
    unnamed x17 -> x18, local copies, waits for them, and re-layouts: 1.24 us -> 6.65 us
  transfers between devices with their start and end apart: 6 -> 0, of which waited for: 1 -> 0; matrix products, arithmetic and copies ran while one was open for 42% -> 0% of each run, Pallas kernels for 0% -> 0%
where the time goes in v1:
time: 57.4 us; the launch traced here: 57 us
  Pallas kernels  47 us (82%)
  local copies, waits for them, and re-layouts  7.24 us (13%)
  other arithmetic  2.06 us (4%)
  between operations  0.7 us (1%)
    pallas_call x1, Pallas kernels, per_device(): pl.pallas_call(functools.partial(kernel, cfg), name='krylov', out_shape=(...  47 us
    unnamed x18, local copies, waits for them, and re-layouts  6.65 us
    concatenate x2, other arithmetic, unpacked(): jnp.concatenate([tile[:, :span_count].T, tile[:, 64:64 + vecs]], axis=0)  1.34 us

profile of v1, /device:TPU:0, one launch (start us, length us, event | category | flops | bytes accessed | tf_op | source)
XLA Modules:
  0.0 57.0 jit_solution(11891051657288822608)
XLA Ops:
  0.6 0.0 copy-start.5
  0.6 0.0 copy-start.7
  0.7 0.6 %copy-done.7 = s32[128]{0:T(128)S(1)} copy-done((s32[128]{0:T(128)S(1)}, s32[128]{0:T(128)}, u32[]{:S(2)}) %copy-start.7) | copy-done | bytes 536
  1.3 0.0 copy-start.6
  1.3 0.0 copy-done.5
  1.3 0.6 %copy-done.6 = s32[128]{0:T(128)S(1)} copy-done((s32[128]{0:T(128)S(1)}, s32[128]{0:T(128)}, u32[]{:S(2)}) %copy-start.6) | copy-done | bytes 536
  2.0 0.7 %fusion.5 = s32[128,16]{0,1:T(8,128)S(1)} fusion(s32[128,16]{0,1:T(8,128)S(1)} %copy-done.5, s32[128,16]{0,1:T(8,128)} %param.14, s32[128]{0:T(128)S(1)} %iota_add_fusion, s32[128]{0:T(128)S(1)} %copy-done.6), kind=kLoop, calls=%fused_computation.10 | loop fusion | flops 51200 | bytes 25600 | tf_op jit(solution)/shard_map/jit(_where)/select_n | solution.py:298
  2.7 0.0 copy-start.3
  2.7 0.0 copy-start.4
  2.7 0.1 copy.15
  2.8 0.2 reshape.20.idx_ref
  3.0 0.5 copy-done.3
  3.5 0.0 copy-done.4
  3.6 0.0 copy-start
  3.6 1.2 %copy-done = f32[1,16,16384]{2,1,0:T(8,128)S(1)} copy-done((f32[1,16,16384]{2,1,0:T(8,128)S(1)}, f32[1,16,16384]{2,1,0:T(8,128)}, u32[]{:S(2)}) %copy-start) | copy-done | bytes 1048600
  4.8 0.0 copy-start.1
  4.8 1.0 %copy-done.1 = f32[1,8,16384]{2,1,0:T(8,128)S(1)} copy-done((f32[1,8,16384]{2,1,0:T(8,128)S(1)}, f32[1,8,16384]{2,1,0:T(8,128)}, u32[]{:S(2)}) %copy-start.1) | copy-done | bytes 524312
  5.8 0.0 copy-start.2
  5.8 0.9 %copy-done.2 = bf16[8,128,128]{2,1,0:T(8,128)(2,1)S(1)} copy-done((bf16[8,128,128]{2,1,0:T(8,128)(2,1)S(1)}, bf16[8,128,128]{2,1,0:T(8,128)(2,1)}, u32[]{:S(2)}) %copy-start.2) | copy-done | bytes 262168
  6.8 47.0 %krylov.1 = (f32[1,8,16384]{2,1,0:T(8,128)S(1)}, f32[1,8,16384]{2,1,0:T(8,128)S(1)}, f32[8,128]{1,0:T(8,128)S(1)}, f32[8,128]{1,0:T(8,128)S(1)}) custom-call(f32[1,8,16384]{2,1,0:T(8,128)S(1)} %copy-done.1, f32[1,16,16384]{2,1,0:T(8,128)S(1)} %copy-done, f32[1,16384]{1,0:T(1,128)S(1)} %copy-done.3, bf16[1024,128]{1,0:T(8,128)(2,1)S(1)} %bitcast.7, ...), custom_call_target="tpu_custom_call" | custom-call | tf_op jit(solution)/shard_map/krylov/pallas_call | solution.py:307
  53.8 0.1 slice.13
  53.9 0.1 copy.16
  53.9 0.7 %pad_maximum_fusion = f32[32,8]{0,1:T(8,128)} fusion(f32[8,8]{0,1:T(8,128)S(1)} %copy.16, f32[24,8]{0,1:T(8,128)S(1)} %slice_bitcast_fusion.1), kind=kLoop, calls=%fused_computation.12 | loop fusion | flops 256 | bytes 2048 | tf_op jit(solution)/shard_map/concatenate | solution.py:336
  54.6 0.1 slice.15
  54.7 0.1 copy.17
  54.8 0.7 %pad_maximum_fusion.1 = f32[40,8]{0,1:T(8,128)} fusion(f32[8,8]{0,1:T(8,128)S(1)} %copy.17, f32[32,8]{0,1:T(8,128)S(1)} %slice_bitcast_fusion), kind=kLoop, calls=%fused_computation.13 | loop fusion | flops 320 | bytes 2560 | tf_op jit(solution)/shard_map/concatenate | solution.py:336
  55.4 0.8 %copy.20 = f32[1,8,16384]{2,1,0:T(8,128)} copy(f32[1,8,16384]{2,1,0:T(8,128)S(1)} %get-tuple-element.16) | data formatting | bytes 1048576
  56.2 0.8 %copy.21 = f32[1,8,16384]{2,1,0:T(8,128)} copy(f32[1,8,16384]{2,1,0:T(8,128)S(1)} %get-tuple-element.17) | data formatting | bytes 1048576
  (5 shorter events, 0.0 us)
Async XLA Ops:
  0.6 0.7 %copy-start.5 = (s32[128,16]{0,1:T(8,128)S(1)}, s32[128,16]{0,1:T(8,128)}, u32[]{:S(2)}) copy-start(s32[128,16]{0,1:T(8,128)} %param.15) | copy-start | bytes 24580
  0.6 0.7 %copy-start.7 = (s32[128]{0:T(128)S(1)}, s32[128]{0:T(128)}, u32[]{:S(2)}) copy-start(s32[128]{0:T(128)} %param.17) | copy-start | bytes 1540
  1.3 0.7 %copy-start.6 = (s32[128]{0:T(128)S(1)}, s32[128]{0:T(128)}, u32[]{:S(2)}) copy-start(s32[128]{0:T(128)} %param.16) | copy-start | bytes 1540
  2.7 0.8 %copy-start.3 = (f32[1,16384]{1,0:T(1,128)S(1)}, f32[1,16384]{1,0:T(1,128)}, u32[]{:S(2)}) copy-start(f32[1,16384]{1,0:T(1,128)} %pot_ref.1) | copy-start | bytes 196612
  2.7 0.9 %copy-start.4 = (bf16[2,128,128]{2,1,0:T(8,128)(2,1)S(1)}, bf16[2,128,128]{2,1,0:T(8,128)(2,1)}, u32[]{:S(2)}) copy-start(bf16[2,128,128]{2,1,0:T(8,128)(2,1)} %soc_ref.1) | copy-start | bytes 196612
  3.6 1.2 %copy-start = (f32[1,16,16384]{2,1,0:T(8,128)S(1)}, f32[1,16,16384]{2,1,0:T(8,128)}, u32[]{:S(2)}) copy-start(f32[1,16,16384]{2,1,0:T(8,128)} %basis_ref.1) | copy-start | bytes 3145732
  4.8 1.0 %copy-start.1 = (f32[1,8,16384]{2,1,0:T(8,128)S(1)}, f32[1,8,16384]{2,1,0:T(8,128)}, u32[]{:S(2)}) copy-start(f32[1,8,16384]{2,1,0:T(8,128)} %vec_ref.1) | copy-start | bytes 1572868
  5.8 0.9 %copy-start.2 = (bf16[8,128,128]{2,1,0:T(8,128)(2,1)S(1)}, bf16[8,128,128]{2,1,0:T(8,128)(2,1)}, u32[]{:S(2)}) copy-start(bf16[8,128,128]{2,1,0:T(8,128)(2,1)} %param.12) | copy-start | bytes 786436

commit v2 on v1

--- a/solution.py
+++ b/solution.py
@@ -18,14 +18,58 @@
     )
 
 
+def spread(table, bcast_ref, count, vecs, width):
+    for m in range(count):
+        bcast_ref[m] = jnp.broadcast_to(table[:, vecs + m:vecs + m + 1], (vecs, width))
+
+
+def combine(work_ref, bcast_ref, image_row, span_rows, vecs, width, out_ref, ext_out):
+    step = 4
+    order = [image_row + r for r in range(vecs)] + span_rows
+
+    def cols(tile):
+        return pl.ds(pl.multiple_of(tile * width, width), width)
+
+    def body(chunk, carry):
+        sums = [None] * step
+        for m, r in enumerate(order):
+            coef = bcast_ref[m]
+            for u in range(step):
+                term = coef * work_ref[pl.ds(r, 1), cols(chunk * step + u)]
+                sums[u] = term if sums[u] is None else sums[u] + term
+        for u in range(step):
+            out_ref[:, cols(chunk * step + u)] = sums[u]
+        if ext_out is not None:
+            for u in range(0, step, 2):
+                pair = jnp.concatenate(sums[u:u + 2], axis=0).astype(jnp.bfloat16)
+                at = pl.multiple_of((chunk * step + u) * vecs, 2 * vecs)
+                ext_out[pl.ds(at, 2 * vecs), :] = pair
+        return carry
+    return step, body
+
+
 def kernel(
     cfg,
-    vec_ref, basis_ref, pot_ref, hop_ref, soc_ref, idx_ref,
-    one_ref, two_ref, coef_one_ref, coef_two_ref,
-    ext_ref, other_ref, halo_ref, prod_ref, image_ref, bcast_ref, stage_a_ref, stage_b_ref,
-    link_send, link_recv, a_send, a_recv, b_send, b_recv,
+    vec_hbm, basis_hbm, pot_hbm, hop_hbm, soc_hbm, nbr_hbm, type_hbm, count_hbm, flip_hbm,
+    one_hbm, image_hbm, small_ref,
+    work_ref, bcast_ref, pot_ref, hop_ref, soc_ref, nbr_ref, type_ref, count_ref, fliploc_ref, table_ref, idx_ref,
+    ext_ref, other_ref, halo_ref, prod_ref, stage_a_ref, stage_b_ref,
+    load_sem, link_send, link_recv, a_send, a_recv, b_send, b_recv,
 ):
     dom_total, group_doms, blocks, width, types, slots, vecs, kept, norm = cfg
+    span_one = kept + vecs
+    span_two = span_one + vecs
+    loads = [
+        pltpu.make_async_copy(src, dst, load_sem.at[n])
+        for n, (src, dst) in enumerate([
+            (nbr_hbm, nbr_ref), (type_hbm, type_ref), (count_hbm, count_ref),
+            (flip_hbm, fliploc_ref), (vec_hbm.at[0], work_ref.at[pl.ds(kept, vecs)]),
+            (basis_hbm.at[0], work_ref.at[pl.ds(0, kept)]), (hop_hbm, hop_ref),
+            (pot_hbm, pot_ref), (soc_hbm, soc_ref)])
+    ]
+    for copy in loads:
+        copy.start()
+    table_copy = pltpu.make_async_copy(table_ref, idx_ref, load_sem.at[len(loads)])
     groups = dom_total // group_doms
     group_size = 2 * group_doms
     dom, spin = lax.axis_index("dom"), lax.axis_index("spin")
@@ -113,7 +157,7 @@
         def body(block, carry):
             terms = [pot_ref[pl.ds(0, 1), cols(block)] * field_ref[:, cols(block)]]
             for slot in range(slots + 1):
-                terms.append(prod_ref[idx_ref[block * (slots + 1) + slot]])
+                terms.append(prod_ref[idx_ref[block, slot]])
             while len(terms) > 1:
                 terms = [sum(terms[p:p + 2][1:], terms[p]) for p in range(0, len(terms), 2)]
             image_ref[:, cols(block)] = terms[0]
@@ -157,44 +201,42 @@
         gram = image_gram + high_dot(moved, tall([total_t]), NT) - high_dot(total_t, tall([first_t]), NT)
         table = jnp.where(lane < vecs, gram, jnp.where(lane == row + vecs, 1.0, 0.0))
         table = table - pltpu.roll(total_t, 2 * vecs, 1)
+        lower = jnp.zeros((vecs, width), jnp.float32)
         for j in range(vecs):
             column = jnp.broadcast_to(table[:, j:j + 1], (vecs, width))
             pivot_row = jnp.broadcast_to(table[j:j + 1, :], (vecs, width))
             pivot = jnp.broadcast_to(column[j:j + 1, :], (vecs, width))
             scale = 1.0 / jnp.sqrt(pivot)
+            lower = jnp.where((lane == j) & (row >= j), column * scale, lower)
             pivot_row = pivot_row * scale
             table = jnp.where(
                 row == j, pivot_row, jnp.where(row > j, table - column * scale * pivot_row, table))
-        upper = jnp.where((lane >= row) & (lane < vecs), table, 0.0)
-        for m in range(vecs + span_count):
-            bcast_ref[m] = jnp.broadcast_to(table[:, vecs + m:vecs + m + 1], (vecs, width))
-        return total_t + pltpu.roll(upper, 64, 1)
-
-    def combine(sources, out_ref, ext_out):
-        step = 4
-
-        def body(chunk, carry):
-            sums = [None] * step
-            m = 0
-            for ref, hi in sources:
-                for r in range(hi):
-                    coef = bcast_ref[m]
-                    for u in range(step):
-                        term = coef * ref[pl.ds(r, 1), cols(chunk * step + u)]
-                        sums[u] = term if sums[u] is None else sums[u] + term
-                    m += 1
-            for u in range(step):
-                out_ref[:, cols(chunk * step + u)] = sums[u]
-            if ext_out is not None:
-                for u in range(0, step, 2):
-                    pair = jnp.concatenate(sums[u:u + 2], axis=0).astype(jnp.bfloat16)
-                    at = pl.multiple_of((chunk * step + u) * vecs, 2 * vecs)
-                    ext_out[pl.ds(at, 2 * vecs), :] = pair
-            return carry
-        return step, body
-
-    field, basis = vec_ref.at[0], basis_ref.at[0]
-    one, two = one_ref.at[0], two_ref.at[0]
+        return total_t + pltpu.roll(lower, span_count, 1), table
+
+    basis = work_ref.at[pl.ds(0, kept)]
+    field = work_ref.at[pl.ds(kept, vecs)]
+    one = work_ref.at[pl.ds(span_one, vecs)]
+    image_ref = work_ref.at[pl.ds(span_two, vecs)]
+
+    for copy in loads[:4]:
+        copy.wait()
+    local = lax.broadcasted_iota(jnp.int32, (slots, blocks), 1)
+    slot_at = lax.broadcasted_iota(jnp.int32, (slots, blocks), 0)
+    shift = nbr_ref[...] - (dom * blocks + local) + RANGE
+    total = dom_total * blocks
+    shift = jnp.where(shift < 0, shift + total, shift)
+    shift = jnp.where(shift >= total, shift - total, shift)
+    place = local + shift - RANGE
+    place = jnp.where(
+        place < 0, place + blocks + RANGE, jnp.where(place >= blocks, place + RANGE, place))
+    live = slot_at < count_ref[...]
+    index = jnp.concatenate([
+        jnp.where(live, type_ref[...] * reach + place, zero_tile),
+        jnp.broadcast_to(fliploc_ref[...] - dom * blocks + flip_base, (8, blocks)),
+        jnp.zeros((width - slots - 8, blocks), jnp.int32)], axis=0)
+    table_ref[...] = jnp.clip(index, 0, flip_base + blocks - 1).T
+    table_copy.start()
+    loads[4].wait()
 
     def round_body(pair, carry):
         both = jnp.concatenate([field[:, cols(2 * pair)], field[:, cols(2 * pair + 1)]], axis=0)
@@ -204,9 +246,12 @@
 
     lax.fori_loop(0, blocks // 2, round_body, 0, unroll=4)
     prod_ref[zero_tile] = jnp.zeros((vecs, width), jnp.float32)
+    loads[5].wait()
     low_gram = [gram_rows(basis.at[pl.ds(g * vecs, vecs)], [(basis, (g + 1) * vecs)])
                 for g in range(kept // vecs)]
     low_gram.append(gram_rows(field, [(basis, kept), (field, vecs)]))
+    for copy in loads[6:] + [table_copy]:
+        copy.wait()
     pl.semaphore_wait(barrier, group_size - 1 + groups - 1 + 2)
 
     def apply_and_gram(app, field_ref, extra, sources):
@@ -229,7 +274,6 @@
 
     for copy in link_copies(0):
         copy.start()
-    span_one = kept + vecs
     result, _ = apply_and_gram(0, field, lambda: None, [(basis, kept), (field, vecs)])
     packed = result
     at = span_one + vecs
@@ -246,10 +290,13 @@
     wide_row = lax.broadcasted_iota(jnp.int32, (width, width), 0) // vecs
     wide_lane = lax.broadcasted_iota(jnp.int32, (width, width), 1) // vecs
     span_gram = low + jnp.where(wide_row < wide_lane, low.T, 0.0)
-    coef_one_ref[...] = factor(
+    coefs, table = factor(
         lanes(packed, 0, span_one), lanes(packed, span_one, vecs), span_gram, span_one)
-
-    step, body = combine([(image_ref, vecs), (basis, kept), (field, vecs)], one, ext_ref.at[1])
+    small_ref[pl.ds(0, vecs), :] = coefs
+    spread(table, bcast_ref, vecs + span_one, vecs, width)
+
+    step, body = combine(
+        work_ref, bcast_ref, span_two, list(range(span_one)), vecs, width, one, ext_ref.at[1])
     chunks, edge = blocks // step, RANGE // step
     tail, head, flip = link_copies(1)
     lax.fori_loop(0, edge, body, 0)
@@ -258,22 +305,75 @@
     head.start()
     lax.fori_loop(edge, chunks - edge, body, 0)
     flip.start()
-
-    span_two = span_one + vecs
+    one_out = pltpu.make_async_copy(
+        work_ref.at[pl.ds(span_one, vecs)], one_hbm, load_sem.at[len(loads) + 1])
+    one_out.start()
+
     result, early = apply_and_gram(
         1, one,
         lambda: gram_rows(one, [(basis, kept), (field, vecs), (one, vecs)]),
         [(basis, kept), (field, vecs), (one, vecs)])
+    image_out = pltpu.make_async_copy(
+        work_ref.at[pl.ds(span_two, vecs)], image_hbm, load_sem.at[len(loads) + 2])
+    image_out.start()
     packed = share(1, result + pltpu.roll(early, 64, 1))
     low = jnp.concatenate(
         [jnp.zeros((span_one, width), jnp.float32), lanes(packed, 64, span_two),
          jnp.zeros((width - span_two, width), jnp.float32)], axis=0)
     span_gram = span_gram + low + jnp.where(wide_row < wide_lane, low.T, 0.0)
-    coef_two_ref[...] = factor(
+    coefs, table = factor(
         lanes(packed, 0, span_two), lanes(packed, span_two, vecs), span_gram, span_two)
+    small_ref[pl.ds(vecs, vecs), :] = coefs
+    small_ref[pl.ds(2 * vecs, vecs), :] = table
+    one_out.wait()
+    image_out.wait()
+
+
+def finish(
+    cfg, small_ref, vec_hbm, basis_hbm, one_in_hbm, image_hbm,
+    one_hbm, two_hbm, coef_one_hbm, coef_two_hbm,
+    work_ref, bcast_ref, two_ref, cut_one_ref, cut_two_ref, load_sem, store_sem,
+):
+    _, _, blocks, width, _, _, vecs, kept, _ = cfg
+    span_one = kept + vecs
+    span_two = span_one + vecs
+    pieces = 4
+    step = 4
+    chunks = blocks // step // pieces
+    span = chunks * step * width
+    loads = []
+    for piece in range(pieces):
+        part = pl.ds(piece * span, span)
+        for n, (src, start, count) in enumerate([
+            (basis_hbm.at[0], 0, kept), (vec_hbm.at[0], kept, vecs),
+            (one_in_hbm, span_one, vecs), (image_hbm, span_two, vecs)]):
+            loads.append(pltpu.make_async_copy(
+                src.at[:, part], work_ref.at[pl.ds(start, count), part], load_sem.at[piece, n]))
+            loads[-1].start()
+    cut_one_ref[...] = small_ref[pl.ds(0, vecs), :span_one + vecs]
+    cut_two_ref[...] = small_ref[pl.ds(vecs, vecs), :span_two + vecs]
+    stores = [
+        pltpu.make_async_copy(cut_one_ref, coef_one_hbm, store_sem.at[0]),
+        pltpu.make_async_copy(cut_two_ref, coef_two_hbm, store_sem.at[1])]
+    for copy in stores:
+        copy.start()
+    spread(small_ref[pl.ds(2 * vecs, vecs), :], bcast_ref, vecs + span_two, vecs, width)
     step, body = combine(
-        [(image_ref, vecs), (basis, kept), (field, vecs), (one, vecs)], two, None)
-    lax.fori_loop(0, chunks, body, 0)
+        work_ref, bcast_ref, span_two, list(range(span_two)), vecs, width, two_ref, None)
+    for piece in range(pieces):
+        part = pl.ds(piece * span, span)
+        for copy in loads[4 * piece:4 * piece + 4]:
+            copy.wait()
+        stores.append(pltpu.make_async_copy(
+            work_ref.at[pl.ds(span_one, vecs), part], one_hbm.at[0, :, part],
+            store_sem.at[2 + piece]))
+        stores[-1].start()
+        lax.fori_loop(piece * chunks, (piece + 1) * chunks, body, 0)
+        stores.append(pltpu.make_async_copy(
+            two_ref.at[:, part], two_hbm.at[0, :, part], store_sem.at[2 + pieces + piece]))
+        stores[-1].start()
+    for copy in stores:
+        copy.wait()
 
 
 def per_device(
@@ -285,57 +385,78 @@
     dom_total = lax.axis_size("dom")
     group_doms = 4 if dom_total % 4 == 0 else 1
     groups = dom_total // group_doms
-    block_total = blocks * dom_total
     reach = blocks + 2 * RANGE
     norm = float(2 * blocks * width * dom_total)
-    first_block = lax.axis_index("dom") * blocks
-    local = jnp.arange(blocks, dtype=jnp.int32)
-    offset = (nbr_block - (first_block + local)[:, None] + RANGE) % block_total - RANGE
-    place = local[:, None] + offset
-    place = jnp.where(
-        place < 0, place + blocks + RANGE, jnp.where(place >= blocks, place + RANGE, place))
-    live = jnp.arange(slots, dtype=jnp.int32)[None, :] < nbr_count[:, None]
-    index = jnp.where(live, nbr_type * reach + place, reach * types)
-    index = jnp.concatenate(
-        [index, (flip_block - first_block + reach * types + 1)[:, None]], axis=1).reshape(-1)
     cfg = (dom_total, group_doms, blocks, width, types, slots, vecs, kept, norm)
     count = blocks * width
     rows = blocks * vecs
+    span_one, span_two = kept + vecs, kept + 2 * vecs
     vmem = pl.BlockSpec(memory_space=pltpu.VMEM)
-    f32, bf16 = jnp.float32, jnp.bfloat16
+    hbm = pl.BlockSpec(memory_space=pltpu.HBM)
+    f32, bf16, i32 = jnp.float32, jnp.bfloat16, jnp.int32
     dma = pltpu.SemaphoreType.DMA
-    one, two, coef_one, coef_two = pl.pallas_call(
+    shape = jax.ShapeDtypeStruct
+    limit = 64 * 1000 * 1000
+    one, image, small = pl.pallas_call(
         functools.partial(kernel, cfg),
         name="krylov",
         out_shape=(
-            jax.ShapeDtypeStruct((1, vecs, count), f32),
-            jax.ShapeDtypeStruct((1, vecs, count), f32),
-            jax.ShapeDtypeStruct((vecs, width), f32),
-            jax.ShapeDtypeStruct((vecs, width), f32),
+            shape((vecs, count), f32),
+            shape((vecs, count), f32),
+            shape((3 * vecs, width), f32),
         ),
-        in_specs=[vmem] * 5 + [pl.BlockSpec(memory_space=pltpu.SMEM)],
-        out_specs=(vmem,) * 4,
+        in_specs=[hbm] * 9,
+        out_specs=(hbm, hbm, vmem),
         scratch_shapes=[
+            pltpu.VMEM((span_two + vecs, count), f32),
+            pltpu.VMEM((span_two + vecs, vecs, width), f32),
+            pltpu.VMEM((1, count), f32),
+            pltpu.VMEM((types * width, width), bf16),
+            pltpu.VMEM(soc_table.shape, bf16),
+            pltpu.VMEM((slots, blocks), i32),
+            pltpu.VMEM((slots, blocks), i32),
+            pltpu.VMEM((1, blocks), i32),
+            pltpu.VMEM((1, blocks), i32),
+            pltpu.VMEM((blocks, width), i32),
+            pltpu.SMEM((blocks, width), i32),
             pltpu.VMEM((2, rows, width), bf16),
             pltpu.VMEM((2, rows, width), bf16),
             pltpu.VMEM((2, 2 * RANGE * vecs, width), bf16),
             pltpu.VMEM((reach * types + 1 + blocks, vecs, width), f32),
-            pltpu.VMEM((vecs, count), f32),
-            pltpu.VMEM((kept + 3 * vecs, vecs, width), f32),
             pltpu.VMEM((2, 2 * group_doms, vecs, width), f32),
             pltpu.VMEM((2, groups, vecs, width), f32),
+            dma((12,)),
             dma((2, 3)), dma((2, 3)),
             dma((2, 2 * group_doms)), dma((2, 2 * group_doms)),
             dma((2, groups)), dma((2, groups)),
         ],
         compiler_params=pltpu.CompilerParams(
-            collective_id=0, has_side_effects=True, vmem_limit_bytes=48 * 1024 * 1024),
-    )(vectors, basis, potential, hop_table.reshape(types * width, width), soc_table, index)
-
-    def unpacked(tile, span_count):
-        return jnp.concatenate([tile[:, :span_count].T, tile[:, 64:64 + vecs]], axis=0)
-
-    return one, two, unpacked(coef_one, kept + vecs), unpacked(coef_two, kept + 2 * vecs)
+            collective_id=0, has_side_effects=True, vmem_limit_bytes=limit),
+    )(
+        vectors, basis, potential, hop_table.reshape(types * width, width), soc_table,
+        nbr_block.T, nbr_type.T, nbr_count.reshape(1, blocks), flip_block.reshape(1, blocks))
+    one, two, coef_one, coef_two = pl.pallas_call(
+        functools.partial(finish, cfg),
+        name="finish",
+        out_shape=(
+            shape((1, vecs, count), f32),
+            shape((1, vecs, count), f32),
+            shape((vecs, span_one + vecs), f32),
+            shape((vecs, span_two + vecs), f32),
+        ),
+        in_specs=[vmem] + [hbm] * 4,
+        out_specs=(hbm,) * 4,
+        scratch_shapes=[
+            pltpu.VMEM((span_two + vecs, count), f32),
+            pltpu.VMEM((span_two + vecs, vecs, width), f32),
+            pltpu.VMEM((vecs, count), f32),
+            pltpu.VMEM((vecs, span_one + vecs), f32),
+            pltpu.VMEM((vecs, span_two + vecs), f32),
+            dma((4, 4)), dma((10,)),
+        ],
+        compiler_params=pltpu.CompilerParams(vmem_limit_bytes=limit),
+    )(small, vectors, basis, one, image)
+    return one, two, coef_one.T, coef_two.T
 
 
 def solution(mesh):

time: 57.4 us -> 50.8 us (0.89)
  local copies, waits for them, and re-layouts: 7.24 us -> 0 us
  Pallas kernels: 47 us -> 49.9 us
  other arithmetic: 2.06 us -> 0 us
    unnamed x18 -> x0, local copies, waits for them, and re-layouts: 6.65 us -> none
    pallas_call x0 -> x1, Pallas kernels: none -> 4.99 us  [per_device(): pl.pallas_call(functools.partial(finish, cfg), name='finish', out_shape=(...]
    pallas_call x1, Pallas kernels: 47 us -> 44.9 us  [per_device(): pl.pallas_call(functools.partial(kernel, cfg), name='krylov', out_shape=(...]
    concatenate x3 -> x0, other arithmetic: 1.34 us -> none  [the longest x2 1.34 us: unpacked(): jnp.concatenate([tile[:, :span_count].T, tile[:, 64:64 + vecs]], axis=0)]
    select_n x1 -> x0, other arithmetic: 0.71 us -> none  [per_device(): index = jnp.where(live, nbr_type * reach + place, reach * types)]
where the time goes in v2:
time: 50.8 us; the launch traced here: 50.6 us
  Pallas kernels  49.9 us (98%)
  between operations  0.64 us (1%)
    pallas_call x1, Pallas kernels, per_device(): pl.pallas_call(functools.partial(kernel, cfg), name='krylov', out_shape=(...  44.9 us
    pallas_call x1, Pallas kernels, per_device(): pl.pallas_call(functools.partial(finish, cfg), name='finish', out_shape=(...  4.99 us

profile of v2, /device:TPU:0, one launch (start us, length us, event | category | flops | bytes accessed | tf_op | source)
XLA Modules:
  0.0 50.6 jit_solution(8675415930085793701)
XLA Ops:
  0.6 44.9 %krylov.1 = (f32[8,16384]{1,0:T(8,128)}, f32[8,16384]{1,0:T(8,128)}, f32[24,128]{1,0:T(8,128)}) custom-call(f32[1,8,16384]{2,1,0:T(8,128)} %vec_hbm.3, f32[1,16,16384]{2,1,0:T(8,128)} %basis_hbm.3, f32[1,16384]{1,0:T(1,128)} %pot_hbm.1, bf16[1024,128]{1,0:T(8,128)(2,1)} %bitcast.7, bf16[2,128,128]{2,1,0:T(8,128)(2,1)} %soc_hbm.1, s32[16,128]{1,0:T(8,128)} %bitcast.8, ...), custom_call_target="tpu_custom_call" | custom-call | tf_op jit(solution)/shard_map/krylov/pallas_call | solution.py:400
  45.6 5.0 %finish.1 = (f32[1,8,16384]{2,1,0:T(8,128)}, f32[1,8,16384]{2,1,0:T(8,128)}, f32[8,32]{1,0:T(8,128)}, f32[8,40]{1,0:T(8,128)}) custom-call(f32[24,128]{1,0:T(8,128)} %get-tuple-element.11.small_ref, f32[1,8,16384]{2,1,0:T(8,128)} %vec_hbm.3, f32[1,16,16384]{2,1,0:T(8,128)} %basis_hbm.3, f32[8,16384]{1,0:T(8,128)} %get-tuple-element.12.one_in_hbm, ...), custom_call_target="tpu_custom_call" | custom-call | tf_op jit(solution)/shard_map/finish/pallas_call | solution.py:438

commit v3 on v2

--- a/solution.py
+++ b/solution.py
@@ -18,41 +18,46 @@
     )
 
 
-def spread(table, bcast_ref, count, vecs, width):
-    for m in range(count):
-        bcast_ref[m] = jnp.broadcast_to(table[:, vecs + m:vecs + m + 1], (vecs, width))
-
-
-def combine(work_ref, bcast_ref, image_row, span_rows, vecs, width, out_ref, ext_out):
-    step = 4
-    order = [image_row + r for r in range(vecs)] + span_rows
-
-    def cols(tile):
-        return pl.ds(pl.multiple_of(tile * width, width), width)
-
-    def body(chunk, carry):
-        sums = [None] * step
-        for m, r in enumerate(order):
-            coef = bcast_ref[m]
-            for u in range(step):
-                term = coef * work_ref[pl.ds(r, 1), cols(chunk * step + u)]
-                sums[u] = term if sums[u] is None else sums[u] + term
-        for u in range(step):
-            out_ref[:, cols(chunk * step + u)] = sums[u]
+def halves(value):
+    top = value.astype(jnp.bfloat16)
+    return top, (value - top.astype(jnp.float32)).astype(jnp.bfloat16)
+
+
+def arranged(table, span_count, image_row, vecs, width):
+    lane = lax.broadcasted_iota(jnp.int32, (vecs, width), 1)
+    spans = jnp.where(lane < span_count, pltpu.roll(table, width - 2 * vecs, 1), 0.0)
+    images = (lane >= image_row) & (lane < image_row + vecs)
+    return (spans + jnp.where(images, pltpu.roll(table, image_row - vecs, 1), 0.0))[
+        :, :image_row + vecs]
+
+
+def combine(work_ref, coefs, vecs, width, chunk, out_ref, ext_out):
+    count = coefs.shape[1]
+    ours_top, ours_rest = halves(coefs)
+
+    def dot(left, right):
+        return lax.dot_general(left, right, NN, preferred_element_type=jnp.float32)
+
+    def body(piece, carry):
+        part = pl.ds(pl.multiple_of(piece * chunk, chunk), chunk)
+        top, rest = halves(work_ref[pl.ds(0, count), part])
+        out = (dot(ours_top, rest) + dot(ours_rest, top)) + dot(ours_top, top)
+        out_ref[:, part] = out
         if ext_out is not None:
-            for u in range(0, step, 2):
-                pair = jnp.concatenate(sums[u:u + 2], axis=0).astype(jnp.bfloat16)
-                at = pl.multiple_of((chunk * step + u) * vecs, 2 * vecs)
-                ext_out[pl.ds(at, 2 * vecs), :] = pair
+            held = chunk // width
+            stacked = jnp.concatenate(
+                [out[:, u * width:(u + 1) * width] for u in range(held)], axis=0)
+            at = pl.multiple_of(piece * held * vecs, held * vecs)
+            ext_out[pl.ds(at, held * vecs), :] = stacked.astype(jnp.bfloat16)
         return carry
-    return step, body
+    return body
 
 
 def kernel(
     cfg,
     vec_hbm, basis_hbm, pot_hbm, hop_hbm, soc_hbm, nbr_hbm, type_hbm, count_hbm, flip_hbm,
     one_hbm, image_hbm, small_ref,
-    work_ref, bcast_ref, pot_ref, hop_ref, soc_ref, nbr_ref, type_ref, count_ref, fliploc_ref, table_ref, idx_ref,
+    work_ref, pot_ref, hop_ref, soc_ref, nbr_ref, type_ref, count_ref, fliploc_ref, table_ref, idx_ref,
     ext_ref, other_ref, halo_ref, prod_ref, stage_a_ref, stage_b_ref,
     load_sem, link_send, link_recv, a_send, a_recv, b_send, b_recv,
 ):
@@ -122,21 +127,21 @@
             device_id=(dom, 1 - spin), device_id_type=MESH)
         return tail, head, flip
 
-    def gram_rows(left_ref, sources):
-        count = sum(hi for _, hi in sources)
-
-        def body(tile, sums):
-            ours = left_ref[:, cols(tile)]
-            picked = [ref[pl.ds(m, 1), cols(tile)] for ref, hi in sources for m in range(hi)]
-            return tuple(total + ours * one for total, one in zip(sums, picked))
-
-        sums = lax.fori_loop(
-            0, blocks, body, tuple(jnp.zeros((vecs, width), jnp.float32) for _ in range(count)),
-            unroll=2)
-        out = jnp.zeros((vecs, width), jnp.float32)
-        for m, total in enumerate(sums):
-            out = jnp.where(lane == m, jnp.sum(total, axis=1, keepdims=True), out)
-        return out
+    def gram_rows(start, rows, count):
+        chunk = 2048
+
+        def dot(left, right):
+            return lax.dot_general(left, right, NT, preferred_element_type=jnp.float32)
+
+        def body(piece, total):
+            part = pl.ds(pl.multiple_of(piece * chunk, chunk), chunk)
+            ours_top, ours_rest = halves(work_ref[pl.ds(start, rows), part])
+            top, rest = halves(work_ref[pl.ds(0, count), part])
+            return total + (dot(ours_top, rest) + dot(ours_rest, top)) + dot(ours_top, top)
+
+        out = lax.fori_loop(
+            0, blocks * width // chunk, body, jnp.zeros((rows, count), jnp.float32))
+        return jnp.concatenate([out, jnp.zeros((rows, width - count), jnp.float32)], axis=1)
 
     def products(source, count, first):
         def body(pair, carry):
@@ -236,6 +241,7 @@
         jnp.zeros((width - slots - 8, blocks), jnp.int32)], axis=0)
     table_ref[...] = jnp.clip(index, 0, flip_base + blocks - 1).T
     table_copy.start()
+    one[...] = jnp.zeros(one.shape, jnp.float32)
     loads[4].wait()
 
     def round_body(pair, carry):
@@ -247,14 +253,14 @@
     lax.fori_loop(0, blocks // 2, round_body, 0, unroll=4)
     prod_ref[zero_tile] = jnp.zeros((vecs, width), jnp.float32)
     loads[5].wait()
-    low_gram = [gram_rows(basis.at[pl.ds(g * vecs, vecs)], [(basis, (g + 1) * vecs)])
-                for g in range(kept // vecs)]
-    low_gram.append(gram_rows(field, [(basis, kept), (field, vecs)]))
+    whole = gram_rows(0, span_one, span_one)
+    low_gram = [jnp.where(lane < (g + 1) * vecs, whole[g * vecs:(g + 1) * vecs, :], 0.0)
+                for g in range(span_one // vecs)]
     for copy in loads[6:] + [table_copy]:
         copy.wait()
     pl.semaphore_wait(barrier, group_size - 1 + groups - 1 + 2)
 
-    def apply_and_gram(app, field_ref, extra, sources):
+    def apply_and_gram(app, field_ref, extra):
         tail, head, flip = link_copies(app)
         products(ext_ref.at[app], blocks, 0)
         early = extra()
@@ -266,7 +272,7 @@
         products(halo_ref.at[app], 2 * RANGE, blocks)
         gather(field_ref, 0, RANGE)
         gather(field_ref, blocks - RANGE, blocks)
-        result = gram_rows(image_ref, sources + [(image_ref, vecs)])
+        result = gram_rows(span_two, vecs, span_two + vecs)
         tail.wait_send()
         head.wait_send()
         flip.wait_send()
@@ -274,7 +280,9 @@
 
     for copy in link_copies(0):
         copy.start()
-    result, _ = apply_and_gram(0, field, lambda: None, [(basis, kept), (field, vecs)])
+    result, _ = apply_and_gram(0, field, lambda: None)
+    result = jnp.where(lane < span_one, result, jnp.where(
+        lane < span_two, pltpu.roll(result, width - vecs, 1), 0.0))
     packed = result
     at = span_one + vecs
     for g in range(span_one // vecs):
@@ -293,11 +301,11 @@
     coefs, table = factor(
         lanes(packed, 0, span_one), lanes(packed, span_one, vecs), span_gram, span_one)
     small_ref[pl.ds(0, vecs), :] = coefs
-    spread(table, bcast_ref, vecs + span_one, vecs, width)
-
-    step, body = combine(
-        work_ref, bcast_ref, span_two, list(range(span_one)), vecs, width, one, ext_ref.at[1])
-    chunks, edge = blocks // step, RANGE // step
+    chunk = RANGE * width
+    body = combine(
+        work_ref, arranged(table, span_one, span_two, vecs, width), vecs, width, chunk, one,
+        ext_ref.at[1])
+    chunks, edge = blocks // RANGE, 1
     tail, head, flip = link_copies(1)
     lax.fori_loop(0, edge, body, 0)
     lax.fori_loop(chunks - edge, chunks, body, 0)
@@ -311,8 +319,7 @@
 
     result, early = apply_and_gram(
         1, one,
-        lambda: gram_rows(one, [(basis, kept), (field, vecs), (one, vecs)]),
-        [(basis, kept), (field, vecs), (one, vecs)])
+        lambda: gram_rows(span_one, vecs, span_two))
     image_out = pltpu.make_async_copy(
         work_ref.at[pl.ds(span_two, vecs)], image_hbm, load_sem.at[len(loads) + 2])
     image_out.start()
@@ -332,15 +339,15 @@
 def finish(
     cfg, small_ref, vec_hbm, basis_hbm, one_in_hbm, image_hbm,
     one_hbm, two_hbm, coef_one_hbm, coef_two_hbm,
-    work_ref, bcast_ref, two_ref, cut_one_ref, cut_two_ref, load_sem, store_sem,
+    work_ref, two_ref, cut_one_ref, cut_two_ref, load_sem, store_sem,
 ):
     _, _, blocks, width, _, _, vecs, kept, _ = cfg
     span_one = kept + vecs
     span_two = span_one + vecs
     pieces = 4
-    step = 4
-    chunks = blocks // step // pieces
-    span = chunks * step * width
+    chunk = RANGE * width
+    chunks = blocks // RANGE // pieces
+    span = chunks * chunk
     loads = []
     for piece in range(pieces):
         part = pl.ds(piece * span, span)
@@ -357,9 +364,10 @@
         pltpu.make_async_copy(cut_two_ref, coef_two_hbm, store_sem.at[1])]
     for copy in stores:
         copy.start()
-    spread(small_ref[pl.ds(2 * vecs, vecs), :], bcast_ref, vecs + span_two, vecs, width)
-    step, body = combine(
-        work_ref, bcast_ref, span_two, list(range(span_two)), vecs, width, two_ref, None)
+    body = combine(
+        work_ref,
+        arranged(small_ref[pl.ds(2 * vecs, vecs), :], span_two, span_two, vecs, width),
+        vecs, width, chunk, two_ref, None)
     for piece in range(pieces):
         part = pl.ds(piece * span, span)
         for copy in loads[4 * piece:4 * piece + 4]:
@@ -409,7 +417,6 @@
         out_specs=(hbm, hbm, vmem),
         scratch_shapes=[
             pltpu.VMEM((span_two + vecs, count), f32),
-            pltpu.VMEM((span_two + vecs, vecs, width), f32),
             pltpu.VMEM((1, count), f32),
             pltpu.VMEM((types * width, width), bf16),
             pltpu.VMEM(soc_table.shape, bf16),
@@ -448,7 +455,6 @@
         out_specs=(hbm,) * 4,
         scratch_shapes=[
             pltpu.VMEM((span_two + vecs, count), f32),
-            pltpu.VMEM((span_two + vecs, vecs, width), f32),
             pltpu.VMEM((vecs, count), f32),
             pltpu.VMEM((vecs, span_one + vecs), f32),
             pltpu.VMEM((vecs, span_two + vecs), f32),

time: 50.8 us -> 51.6 us (1.016)
  Pallas kernels: 49.9 us -> 50.6 us
where the time goes in v3:
time: 51.6 us; the launch traced here: 51.3 us
  Pallas kernels  50.6 us (98%)
  between operations  0.64 us (1%)
    pallas_call x1, Pallas kernels, per_device(): pl.pallas_call(functools.partial(kernel, cfg), name='krylov', out_shape=(...  45.3 us
    pallas_call x1, Pallas kernels, per_device(): pl.pallas_call(functools.partial(finish, cfg), name='finish', out_shape=(...  5.39 us

profile of v3, /device:TPU:0, one launch (start us, length us, event | category | flops | bytes accessed | tf_op | source)
XLA Modules:
  0.0 51.3 jit_solution(3517608273865390823)
XLA Ops:
  0.6 45.3 %krylov.1 = (f32[8,16384]{1,0:T(8,128)}, f32[8,16384]{1,0:T(8,128)}, f32[24,128]{1,0:T(8,128)}) custom-call(f32[1,8,16384]{2,1,0:T(8,128)} %vec_hbm.3, f32[1,16,16384]{2,1,0:T(8,128)} %basis_hbm.3, f32[1,16384]{1,0:T(1,128)} %pot_hbm.1, bf16[1024,128]{1,0:T(8,128)(2,1)} %bitcast.7, bf16[2,128,128]{2,1,0:T(8,128)(2,1)} %soc_hbm.1, s32[16,128]{1,0:T(8,128)} %bitcast.8, ...), custom_call_target="tpu_custom_call" | custom-call | tf_op jit(solution)/shard_map/krylov/pallas_call | solution.py:408
  45.9 5.4 %finish.1 = (f32[1,8,16384]{2,1,0:T(8,128)}, f32[1,8,16384]{2,1,0:T(8,128)}, f32[8,32]{1,0:T(8,128)}, f32[8,40]{1,0:T(8,128)}) custom-call(f32[24,128]{1,0:T(8,128)} %get-tuple-element.11.small_ref, f32[1,8,16384]{2,1,0:T(8,128)} %vec_hbm.3, f32[1,16,16384]{2,1,0:T(8,128)} %basis_hbm.3, f32[8,16384]{1,0:T(8,128)} %get-tuple-element.12.one_in_hbm, ...), custom_call_target="tpu_custom_call" | custom-call | tf_op jit(solution)/shard_map/finish/pallas_call | solution.py:445

commit v4 on v2

--- a/solution.py
+++ b/solution.py
@@ -246,13 +246,15 @@
 
     lax.fori_loop(0, blocks // 2, round_body, 0, unroll=4)
     prod_ref[zero_tile] = jnp.zeros((vecs, width), jnp.float32)
+    pl.semaphore_wait(barrier, group_size - 1 + groups - 1 + 2)
+    for copy in link_copies(0):
+        copy.start()
     loads[5].wait()
     low_gram = [gram_rows(basis.at[pl.ds(g * vecs, vecs)], [(basis, (g + 1) * vecs)])
                 for g in range(kept // vecs)]
     low_gram.append(gram_rows(field, [(basis, kept), (field, vecs)]))
     for copy in loads[6:] + [table_copy]:
         copy.wait()
-    pl.semaphore_wait(barrier, group_size - 1 + groups - 1 + 2)
 
     def apply_and_gram(app, field_ref, extra, sources):
         tail, head, flip = link_copies(app)
@@ -272,8 +274,6 @@
         flip.wait_send()
         return result, early
 
-    for copy in link_copies(0):
-        copy.start()
     result, _ = apply_and_gram(0, field, lambda: None, [(basis, kept), (field, vecs)])
     packed = result
     at = span_one + vecs

time: 50.8 us -> 51.8 us (1.020)
  Pallas kernels: 49.9 us -> 50.8 us
    pallas_call x1, Pallas kernels: 44.9 us -> 45.8 us  [per_device(): pl.pallas_call(functools.partial(kernel, cfg), name='krylov', out_shape=(...]
where the time goes in v4:
time: 51.8 us; the launch traced here: 51.5 us
  Pallas kernels  50.8 us (98%)
  between operations  0.64 us (1%)
    pallas_call x1, Pallas kernels, per_device(): pl.pallas_call(functools.partial(kernel, cfg), name='krylov', out_shape=(...  45.8 us
    pallas_call x1, Pallas kernels, per_device(): pl.pallas_call(functools.partial(finish, cfg), name='finish', out_shape=(...  4.99 us

profile of v4, /device:TPU:0, one launch (start us, length us, event | category | flops | bytes accessed | tf_op | source)
XLA Modules:
  0.0 51.5 jit_solution(16081668264703425920)
XLA Ops:
  0.6 45.8 %krylov.1 = (f32[8,16384]{1,0:T(8,128)}, f32[8,16384]{1,0:T(8,128)}, f32[24,128]{1,0:T(8,128)}) custom-call(f32[1,8,16384]{2,1,0:T(8,128)} %vec_hbm.3, f32[1,16,16384]{2,1,0:T(8,128)} %basis_hbm.3, f32[1,16384]{1,0:T(1,128)} %pot_hbm.1, bf16[1024,128]{1,0:T(8,128)(2,1)} %bitcast.7, bf16[2,128,128]{2,1,0:T(8,128)(2,1)} %soc_hbm.1, s32[16,128]{1,0:T(8,128)} %bitcast.8, ...), custom_call_target="tpu_custom_call" | custom-call | tf_op jit(solution)/shard_map/krylov/pallas_call | solution.py:400
  46.5 5.0 %finish.1 = (f32[1,8,16384]{2,1,0:T(8,128)}, f32[1,8,16384]{2,1,0:T(8,128)}, f32[8,32]{1,0:T(8,128)}, f32[8,40]{1,0:T(8,128)}) custom-call(f32[24,128]{1,0:T(8,128)} %get-tuple-element.11.small_ref, f32[1,8,16384]{2,1,0:T(8,128)} %vec_hbm.3, f32[1,16,16384]{2,1,0:T(8,128)} %basis_hbm.3, f32[8,16384]{1,0:T(8,128)} %get-tuple-element.12.one_in_hbm, ...), custom_call_target="tpu_custom_call" | custom-call | tf_op jit(solution)/shard_map/finish/pallas_call | solution.py:438
